TPU v7x, 32 devices: a whole 2x2x4 slice. The times are simulated.
32 devices in a mesh: gx: 8 (over y, x, core), gy: 4 (over z).
Axes of the slice: x: 2, y: 2, z: 4, core: 2. Of those that a mesh axis runs over, the one named last changes fastest.
Arguments:
- estimate: float32 [128, 64, 128], P('gx', 'gy'), may hold values from -6 to 6
- measured: float32 [128, 64, 128], P('gx', 'gy'), may hold values from -6 to 6
- weights: float32 [4, 128, 64, 128], P(None, 'gx', 'gy'), may hold values from 0.3 to 3
- kernels: float32 [4, 3, 15], replicated, may hold values from -0.6 to 0.6
- step_size: float32 [1], replicated, may hold values from 0.1 to 0.25
- penalty: float32 [1], replicated, may hold values from 0.2 to 1
Outputs:
- current: float32 [128, 64, 128], P('gx', 'gy')
- extrapolated: float32 [128, 64, 128], P('gx', 'gy')
All inputs are finite; a program needn't handle non-finite values.
Results may differ from a plain program's by a relative error of at most 0.0003.
Values sent between devices are 32-bit elements; how exact they have to be, the bound alone decides.
A program may use at most 64 MiB of HBM per device.

v0:
```python
import functools
import math

import jax
import jax.numpy as jnp
from jax import lax
from jax.experimental import pallas as pl
from jax.experimental.pallas import tpu as pltpu
from jax.sharding import PartitionSpec as P

ITERS = 2
SUBLANES = 8
MESH = pl.DeviceIdType.MESH
SIDES = [(0, -1), (0, 1), (-1, 0), (1, 0), (-1, -1), (-1, 1), (1, -1), (1, 1)]
F32 = jnp.float32
BF16 = jnp.bfloat16


def log2(n):
    assert n & (n - 1) == 0
    return n.bit_length() - 1


def split(value):
    high = value.astype(BF16)
    low = (value - high.astype(F32)).astype(BF16)
    return high, low


def kernel(
    nx, ny, rows, cols, depth, taps, ranks,
    k_ref, step_ref, pen_ref, est_ref, meas_ref, w_ref,
    cur_ref, ext_ref,
    x_ref, m_ref, wv_ref, hz, hx, hc, gz, gx_, gc,
    a0, a1, b0, b1, sf, sa, zf, za, acc, v_ref,
    local_sem, send_sem, recv_sem,
):
    margin = taps // 2
    wide = -(-margin // SUBLANES) * SUBLANES
    tall = -(-margin // SUBLANES) * SUBLANES
    own = rows * cols
    gx = lax.axis_index("gx")
    gy = lax.axis_index("gy")

    def there(side):
        ok = None
        for at, by, count in ((gx, side[0], nx), (gy, side[1], ny)):
            if by == 0:
                continue
            one = (at + by >= 0) & (at + by < count)
            ok = one if ok is None else ok & one
        return ok

    def slot(bufs, lead, side):
        z, x, c = bufs
        n = SIDES.index(side)
        if n < 2:
            return z.at[lead, n]
        if n < 4:
            return x.at[lead, n - 2, pl.ds(0, margin)]
        return c.at[lead, n - 4, pl.ds(0, margin)]

    def edge(ref, side):
        dx, dy = side
        r = {0: (0, rows), -1: (0, margin), 1: (rows - margin, margin)}[dx]
        c = {0: (0, cols), -1: (0, wide), 1: (cols - wide, wide)}[dy]
        return ref.at[pl.ds(*r), pl.ds(*c)]

    halo = (hz, hx, hc)

    def transfer(phase, side, src):
        back = (-side[0], -side[1])
        return pltpu.make_async_remote_copy(
            src_ref=src,
            dst_ref=slot(halo, phase, back),
            send_sem=send_sem.at[phase, SIDES.index(side)],
            recv_sem=recv_sem.at[phase, SIDES.index(back)],
            device_id=(gx + side[0], gy + side[1]),
            device_id_type=MESH,
        )

    def source(phase, side):
        if phase % 2 == 1:
            return slot((gz, gx_, gc), phase // 2, side)
        return edge(est_ref if phase == 0 else x_ref, side)

    def send(phase, sides):
        for side in sides:
            @pl.when(there(side))
            def _():
                transfer(phase, side, source(phase, side)).start()

    def receive(phase, sides):
        for side in sides:
            back = (-side[0], -side[1])

            @pl.when(there(side))
            def _():
                transfer(phase, back, source(phase, back)).wait_recv()

    copies = [
        pltpu.make_async_copy(est_ref, x_ref, local_sem.at[0]),
        pltpu.make_async_copy(meas_ref, m_ref, local_sem.at[1]),
        pltpu.make_async_copy(w_ref, wv_ref, local_sem.at[2]),
    ]
    for copy in copies:
        copy.start()

    barrier = pltpu.get_barrier_semaphore()
    near = 0
    for side in SIDES:
        @pl.when(there(side))
        def _():
            pl.semaphore_signal(
                barrier, inc=1, device_id=(gx + side[0], gy + side[1]), device_id_type=MESH
            )
        near = near + there(side).astype(jnp.int32)
    pl.semaphore_wait(barrier, near)
    order = SIDES[4:] + SIDES[:4]
    send(0, order)

    for phase in range(2 * ITERS):
        for n in range(2):
            hx[phase, n, margin:] = jnp.zeros((tall - margin, cols, depth), F32)
        for n in range(4):
            hc[phase, n, margin:] = jnp.zeros((tall - margin, wide, depth), F32)
        for side in SIDES:
            @pl.when(jnp.logical_not(there(side)))
            def _():
                ref = slot(halo, phase, side)
                ref[...] = jnp.zeros(ref.shape, F32)

    tile = own

    def places(t, shape, dim):
        at = lax.broadcasted_iota(jnp.int32, shape, dim)
        if t == 0:
            return at >> log2(cols), at & (cols - 1)
        if t == 1:
            half = rows * wide
            p = (at & (half - 1)) >> log2(wide)
            q = at & (wide - 1)
            return p, jnp.where(at >= half, q + cols, q - wide)
        if t == 2:
            half = tall * cols
            p = (at & (half - 1)) >> log2(cols)
            q = at & (cols - 1)
            return jnp.where(at >= half, p + rows, p - margin), q
        part = tall * wide
        n = at >> log2(part)
        p = (at & (part - 1)) >> log2(wide)
        q = at & (wide - 1)
        return (
            jnp.where(n >= 2, p + rows, p - margin),
            jnp.where((n & 1) == 1, q + cols, q - wide),
        )

    def banded(gap, m, axis):
        out = jnp.zeros(gap.shape, F32)
        for t in range(taps):
            out = jnp.where(gap == t, k_ref[m, axis, t], out)
        return out

    for t in range(4):
        shape = (rows, tile)
        p, q = places(t, shape, 1)
        gap_p = p - lax.broadcasted_iota(jnp.int32, shape, 0) + margin
        gap_q = q - lax.broadcasted_iota(jnp.int32, (cols, tile), 0) + margin

        def table(m, _):
            a0[m, :, t * tile:(t + 1) * tile] = banded(gap_p, m, 0)
            a1[m, :, t * tile:(t + 1) * tile] = banded(gap_q, m, 1)
            return 0

        lax.fori_loop(0, ranks, table, 0)

    def fill_forward(u, _):
        m, i = u >> log2(rows), u & (rows - 1)
        at = pl.ds(pl.multiple_of(u * cols, cols), cols)
        for t in range(4):
            span = slice(t * tile, (t + 1) * tile)
            high, low = split(a0[m, pl.ds(i, 1), span] * a1[m, :, span])
            sf[at, 2 * t * tile:(2 * t + 1) * tile] = high
            sf[at, (2 * t + 1) * tile:(2 * t + 2) * tile] = low
        return 0

    lax.fori_loop(0, ranks * rows, fill_forward, 0)

    gap_z = (
        lax.broadcasted_iota(jnp.int32, (depth, depth), 0)
        - lax.broadcasted_iota(jnp.int32, (depth, depth), 1)
        + margin
    )

    def optical(m, _):
        for ref, gap in ((zf, gap_z), (za, 2 * margin - gap_z)):
            high, low = split(banded(gap, m, 2))
            ref[m, :depth, :depth] = high
            ref[m, :depth, depth:] = low
            ref[m, depth:, :depth] = high
            ref[m, depth:, depth:] = jnp.zeros((depth, depth), BF16)
        return 0

    lax.fori_loop(0, ranks, optical, 0)

    lane_i, lane_j = places(0, (b0.shape[1], tile), 1)
    gap_i = lax.broadcasted_iota(jnp.int32, lane_i.shape, 0) - lane_i
    gap_j = lax.broadcasted_iota(jnp.int32, lane_j.shape, 0) - wide - lane_j + margin

    def table_back(m, _):
        b0[m] = banded(gap_i, m, 0)
        b1[m] = banded(gap_j, m, 1)
        return 0

    lax.fori_loop(0, ranks, table_back, 0)

    def put(start, first, qs):
        at = pl.ds(pl.multiple_of(start, 2 * SUBLANES), 2 * SUBLANES)
        for m in range(ranks):
            cells = [b0[m, pl.ds(f, 1), :] * b1[m, qs, :] for f in first]
            cells = cells[0] if len(cells) == 1 else jnp.concatenate(cells, 0)
            high, low = split(cells)
            sa[at, 2 * m * tile:(2 * m + 1) * tile] = high
            sa[at, (2 * m + 1) * tile:(2 * m + 2) * tile] = low

    middle = slice(wide, wide + cols)
    flanks = (slice(0, wide), slice(wide + cols, wide + cols + wide))

    def fill_own(p, _):
        put(p * cols, (p + margin,), middle)
        return 0

    def fill_z(u, _):
        for n in range(2):
            put(tile + n * rows * wide + u * 2 * wide, (2 * u + margin, 2 * u + 1 + margin), flanks[n])
        return 0

    def fill_x(u, _):
        for n in range(2):
            put(2 * tile + n * tall * cols + u * cols, (u + n * (rows + margin),), middle)
        return 0

    def fill_c(u, _):
        for n in range(4):
            first = 2 * u + (n // 2) * (rows + margin)
            put(3 * tile + n * tall * wide + u * 2 * wide, (first, first + 1), flanks[n % 2])
        return 0

    lax.fori_loop(0, rows, fill_own, 0)
    lax.fori_loop(0, rows // 2, fill_z, 0)
    lax.fori_loop(0, tall, fill_x, 0)
    lax.fori_loop(0, tall // 2, fill_c, 0)

    for copy in copies:
        copy.wait()

    step = step_ref[0]
    shrink = step * pen_ref[0]
    groups = [None, SIDES[0:2], SIDES[2:4], SIDES[4:8]]

    def doubled(cells):
        return jnp.concatenate([jnp.concatenate(split(cells), 1)] * 2, 0)

    def both(pair):
        return pair[:, :depth] + pair[:, depth:]

    momentum = 1.0
    for iteration in range(ITERS):
        phase = 2 * iteration
        for t in range(4):
            if t == 0:
                cells = x_ref[...]
            else:
                receive(phase, groups[t])
                cells = halo[t - 1][phase]
            right = doubled(cells.reshape(tile, depth))
            for m in range(ranks):
                at = slice(m * own, (m + 1) * own)
                part = jnp.dot(
                    sf[at, 2 * t * tile:(2 * t + 2) * tile], right, preferred_element_type=F32
                )
                acc[at] = part if t == 0 else acc[at] + part
        residual = -m_ref[...].reshape(own, depth)
        for m in range(ranks):
            at = slice(m * own, (m + 1) * own)
            mixed = jnp.concatenate(split(both(acc[at])), 1)
            blurred = both(jnp.dot(mixed, zf[m], preferred_element_type=F32))
            residual = residual + wv_ref[m].reshape(own, depth) * blurred
        for m in range(ranks):
            mixed = jnp.concatenate(split(wv_ref[m].reshape(own, depth) * residual), 1)
            back = both(jnp.dot(mixed, za[m], preferred_element_type=F32))
            v_ref[2 * m * tile:(2 * m + 2) * tile] = doubled(back)

        def spread(t):
            return both(
                jnp.dot(sa[t * tile:(t + 1) * tile], v_ref[...], preferred_element_type=F32)
            )

        phase = phase + 1
        outgoing = (gz, gx_, gc)
        for t in (3, 1, 2):
            ref = outgoing[t - 1]
            ref[iteration] = spread(t).reshape(ref.shape[1:])
            send(phase, groups[t])
        acc[:own, :depth] = spread(0)
        grad = acc.at[:own, :depth]
        receive(phase, SIDES)
        total = grad[...].reshape(rows, cols, depth)
        inner = jnp.concatenate(
            [hz[phase, 0], hz[phase, 1]], 1
        ) if cols == 2 * wide else None
        total = total + inner
        lower = jnp.concatenate([hc[phase, 0], hc[phase, 1]], 1) + hx[phase, 0]
        upper = jnp.concatenate([hc[phase, 2], hc[phase, 3]], 1) + hx[phase, 1]
        lower = lower[:margin]
        upper = upper[:margin]
        gap = jnp.zeros((rows - margin, cols, depth), F32)
        total = total + jnp.concatenate([lower, gap], 0) + jnp.concatenate([gap, upper], 0)
        extrapolated = x_ref[...]
        current = extrapolated if iteration == 0 else cur_ref[...]
        moved = extrapolated - step * total
        updated = jnp.where(
            moved > shrink, moved - shrink, jnp.where(moved < -shrink, moved + shrink, 0.0)
        )
        following = (1.0 + math.sqrt(1.0 + 4.0 * momentum * momentum)) / 2.0
        extrapolated = updated + (momentum - 1.0) / following * (updated - current)
        cur_ref[...] = updated
        momentum = following
        if iteration + 1 < ITERS:
            x_ref[...] = extrapolated
            send(phase + 1, order)
        else:
            ext_ref[...] = extrapolated

    for phase in range(2 * ITERS):
        for side in SIDES:
            @pl.when(there(side))
            def _():
                transfer(phase, side, source(phase, side)).wait_send()


def on_device(nx, ny, estimate, measured, weights, kernels, step_size, penalty):
    rows, cols, depth = estimate.shape
    ranks, _, taps = kernels.shape
    margin = taps // 2
    wide = -(-margin // SUBLANES) * SUBLANES
    tall = wide
    own = rows * cols
    assert cols == 2 * wide and rows == 2 * tall and ITERS >= 1
    phases = 2 * ITERS
    smem = pl.BlockSpec(memory_space=pltpu.SMEM)
    hbm = pl.BlockSpec(memory_space=pl.ANY)
    vmem = pl.BlockSpec(memory_space=pltpu.VMEM)

    def pieces(lead):
        return [
            pltpu.VMEM((lead, 2, rows, wide, depth), F32),
            pltpu.VMEM((lead, 2, tall, cols, depth), F32),
            pltpu.VMEM((lead, 4, tall, wide, depth), F32),
        ]

    out = jax.ShapeDtypeStruct(estimate.shape, F32)
    return pl.pallas_call(
        functools.partial(kernel, nx, ny, rows, cols, depth, taps, ranks),
        out_shape=(out, out),
        in_specs=[smem, smem, smem, hbm, hbm, hbm],
        out_specs=(vmem, vmem),
        scratch_shapes=[
            pltpu.VMEM(estimate.shape, F32),
            pltpu.VMEM(measured.shape, F32),
            pltpu.VMEM(weights.shape, F32),
            *pieces(phases),
            *pieces(ITERS),
            pltpu.VMEM((ranks, rows, 4 * own), F32),
            pltpu.VMEM((ranks, cols, 4 * own), F32),
            pltpu.VMEM((ranks, rows + 2 * tall, own), F32),
            pltpu.VMEM((ranks, cols + 2 * wide, own), F32),
            pltpu.VMEM((ranks * own, 8 * own), BF16),
            pltpu.VMEM((4 * own, 2 * ranks * own), BF16),
            pltpu.VMEM((ranks, 2 * depth, 2 * depth), BF16),
            pltpu.VMEM((ranks, 2 * depth, 2 * depth), BF16),
            pltpu.VMEM((ranks * own, 2 * depth), F32),
            pltpu.VMEM((2 * ranks * own, 2 * depth), BF16),
            pltpu.SemaphoreType.DMA((3,)),
            pltpu.SemaphoreType.DMA((phases, len(SIDES))),
            pltpu.SemaphoreType.DMA((phases, len(SIDES))),
        ],
        compiler_params=pltpu.CompilerParams(collective_id=0, has_side_effects=True),
        name="fista",
    )(kernels, step_size, penalty, estimate, measured, weights)


def solution(mesh):
    return jax.shard_map(
        functools.partial(on_device, mesh.shape["gx"], mesh.shape["gy"]),
        mesh=mesh,
        in_specs=(
            P("gx", "gy", None),
            P("gx", "gy", None),
            P(None, "gx", "gy", None),
            P(),
            P(),
            P(),
        ),
        out_specs=(P("gx", "gy", None), P("gx", "gy", None)),
        check_vma=False,
    )
```

profile of v0, /device:TPU:1, one launch (start us, length us, event | category | flops | bytes accessed | tf_op | source)
XLA Modules:
  0.0 35.1 jit_solution(16721481011626048486)
XLA Ops:
  1.9 1.3 %copy.8.k_ref = f32[4,3,15]{2,1,0:T(4,128)} copy(f32[4,3,15]{2,0,1:T(4,128)} %param.9) | data formatting | bytes 1440 | tf_op args[3]
  3.2 29.6 %fista.1 = (f32[16,16,128]{2,1,0:T(8,128)}, f32[16,16,128]{2,1,0:T(8,128)}) custom-call(f32[4,3,15]{2,1,0:T(4,128)} %copy.8.k_ref, f32[1]{0:T(128)S(6)} %copy.11.step_ref, f32[1]{0:T(128)S(6)} %copy.12.pen_ref, f32[16,16,128]{2,1,0:T(8,128)} %est_ref.1, f32[16,16,128]{2,1,0:T(8,128)} %meas_ref.1, f32[4,16,16,128]{3,2,1,0:T(8,128)} %w_ref.1), custom_call_target="tpu_custom_call" | custom-call | tf_op jit(solution)/shard_map/fista/pallas_call | solution.py:363
  32.9 0.0 copy-start
  32.9 1.6 %copy.13 = f32[16,16,128]{2,1,0:T(8,128)} copy(f32[16,16,128]{2,1,0:T(8,128)} %get-tuple-element.4) | data formatting | bytes 262144
  34.5 0.0 copy-done
  34.5 0.7 %copy.14 = f32[16,16,128]{2,1,0:T(8,128)} copy(f32[16,16,128]{2,1,0:T(8,128)S(1)} %copy-done) | data formatting | bytes 262144
Async XLA Ops:
  32.9 1.6 %copy-start = (f32[16,16,128]{2,1,0:T(8,128)S(1)}, f32[16,16,128]{2,1,0:T(8,128)}, u32[]{:S(2)}) copy-start(f32[16,16,128]{2,1,0:T(8,128)} %get-tuple-element.5) | copy-start | bytes 393220
where the time goes:
time: 35.4 us; the launch traced here: 35.1 us
  Pallas kernels  29.6 us (84%)
  local copies, waits for them, and re-layouts  3.56 us (10%)
  between operations  1.94 us (5%)
    pallas_call x1, Pallas kernels, on_device(): pl.pallas_call(functools.partial(kernel, nx, ny, rows, cols, depth, taps,...  29.6 us
    unnamed x5, local copies, waits for them, and re-layouts  3.56 us

commit v1 on v0

--- a/solution.py
+++ b/solution.py
@@ -21,6 +21,13 @@
     return n.bit_length() - 1
 
 
+def weight_of(iteration):
+    momentum = 1.0
+    for _ in range(iteration + 1):
+        before, momentum = momentum, (1.0 + math.sqrt(1.0 + 4.0 * momentum * momentum)) / 2.0
+    return (before - 1.0) / momentum
+
+
 def split(value):
     high = value.astype(BF16)
     low = (value - high.astype(F32)).astype(BF16)
@@ -30,7 +37,7 @@
 def kernel(
     nx, ny, rows, cols, depth, taps, ranks,
     k_ref, step_ref, pen_ref, est_ref, meas_ref, w_ref,
-    cur_ref, ext_ref,
+    delta_ref, cur_ref,
     x_ref, m_ref, wv_ref, hz, hx, hc, gz, gx_, gc,
     a0, a1, b0, b1, sf, sa, zf, za, acc, v_ref,
     local_sem, send_sem, recv_sem,
@@ -51,19 +58,20 @@
             ok = one if ok is None else ok & one
         return ok
 
-    def slot(bufs, lead, side):
+    def slot(bufs, lead, side, turned=False):
         z, x, c = bufs
         n = SIDES.index(side)
+        q = pl.ds(wide - margin if (side[1] < 0) != turned else 0, margin)
         if n < 2:
-            return z.at[lead, n]
+            return z.at[lead, n, :, q]
         if n < 4:
             return x.at[lead, n - 2, pl.ds(0, margin)]
-        return c.at[lead, n - 4, pl.ds(0, margin)]
+        return c.at[lead, n - 4, pl.ds(0, margin), q]
 
     def edge(ref, side):
         dx, dy = side
         r = {0: (0, rows), -1: (0, margin), 1: (rows - margin, margin)}[dx]
-        c = {0: (0, cols), -1: (0, wide), 1: (cols - wide, wide)}[dy]
+        c = {0: (0, cols), -1: (0, margin), 1: (cols - margin, margin)}[dy]
         return ref.at[pl.ds(*r), pl.ds(*c)]
 
     halo = (hz, hx, hc)
@@ -72,7 +80,7 @@
         back = (-side[0], -side[1])
         return pltpu.make_async_remote_copy(
             src_ref=src,
-            dst_ref=slot(halo, phase, back),
+            dst_ref=slot(halo, phase, back, phase % 2 == 1),
             send_sem=send_sem.at[phase, SIDES.index(side)],
             recv_sem=recv_sem.at[phase, SIDES.index(back)],
             device_id=(gx + side[0], gy + side[1]),
@@ -119,15 +127,19 @@
     order = SIDES[4:] + SIDES[:4]
     send(0, order)
 
+    spare = (slice(0, wide - margin), slice(margin, wide))
     for phase in range(2 * ITERS):
         for n in range(2):
             hx[phase, n, margin:] = jnp.zeros((tall - margin, cols, depth), F32)
+        for n in range(2):
+            hz[phase, n, :, spare[(n + phase) % 2]] = jnp.zeros((rows, wide - margin, depth), F32)
         for n in range(4):
+            hc[phase, n, :, spare[(n + phase) % 2]] = jnp.zeros((tall, wide - margin, depth), F32)
             hc[phase, n, margin:] = jnp.zeros((tall - margin, wide, depth), F32)
         for side in SIDES:
             @pl.when(jnp.logical_not(there(side)))
             def _():
-                ref = slot(halo, phase, side)
+                ref = slot(halo, phase, side, phase % 2 == 1)
                 ref[...] = jnp.zeros(ref.shape, F32)
 
     tile = own
@@ -158,7 +170,7 @@
     def banded(gap, m, axis):
         out = jnp.zeros(gap.shape, F32)
         for t in range(taps):
-            out = jnp.where(gap == t, k_ref[m, axis, t], out)
+            out = jnp.where(gap == t, k_ref[axis, m, t], out)
         return out
 
     for t in range(4):
@@ -214,36 +226,39 @@
 
     lax.fori_loop(0, ranks, table_back, 0)
 
-    def put(start, first, qs):
-        at = pl.ds(pl.multiple_of(start, 2 * SUBLANES), 2 * SUBLANES)
+    def put(t, start, first, qs):
+        at = [
+            pl.ds(pl.multiple_of((2 * t + half) * tile + start, 2 * SUBLANES), 2 * SUBLANES)
+            for half in range(2)
+        ]
         for m in range(ranks):
             cells = [b0[m, pl.ds(f, 1), :] * b1[m, qs, :] for f in first]
             cells = cells[0] if len(cells) == 1 else jnp.concatenate(cells, 0)
             high, low = split(cells)
-            sa[at, 2 * m * tile:(2 * m + 1) * tile] = high
-            sa[at, (2 * m + 1) * tile:(2 * m + 2) * tile] = low
+            sa[at[0], m * own:(m + 1) * own] = high
+            sa[at[1], m * own:(m + 1) * own] = low
 
     middle = slice(wide, wide + cols)
     flanks = (slice(0, wide), slice(wide + cols, wide + cols + wide))
 
     def fill_own(p, _):
-        put(p * cols, (p + margin,), middle)
+        put(0, p * cols, (p + margin,), middle)
         return 0
 
     def fill_z(u, _):
         for n in range(2):
-            put(tile + n * rows * wide + u * 2 * wide, (2 * u + margin, 2 * u + 1 + margin), flanks[n])
+            put(1, n * rows * wide + u * 2 * wide, (2 * u + margin, 2 * u + 1 + margin), flanks[n])
         return 0
 
     def fill_x(u, _):
         for n in range(2):
-            put(2 * tile + n * tall * cols + u * cols, (u + n * (rows + margin),), middle)
+            put(2, n * tall * cols + u * cols, (u + n * (rows + margin),), middle)
         return 0
 
     def fill_c(u, _):
         for n in range(4):
             first = 2 * u + (n // 2) * (rows + margin)
-            put(3 * tile + n * tall * wide + u * 2 * wide, (first, first + 1), flanks[n % 2])
+            put(3, n * tall * wide + u * 2 * wide, (first, first + 1), flanks[n % 2])
         return 0
 
     lax.fori_loop(0, rows, fill_own, 0)
@@ -264,7 +279,6 @@
     def both(pair):
         return pair[:, :depth] + pair[:, depth:]
 
-    momentum = 1.0
     for iteration in range(ITERS):
         phase = 2 * iteration
         for t in range(4):
@@ -289,12 +303,13 @@
         for m in range(ranks):
             mixed = jnp.concatenate(split(wv_ref[m].reshape(own, depth) * residual), 1)
             back = both(jnp.dot(mixed, za[m], preferred_element_type=F32))
-            v_ref[2 * m * tile:(2 * m + 2) * tile] = doubled(back)
+            v_ref[m * own:(m + 1) * own] = jnp.concatenate(split(back), 1)
 
         def spread(t):
-            return both(
-                jnp.dot(sa[t * tile:(t + 1) * tile], v_ref[...], preferred_element_type=F32)
+            sums = jnp.dot(
+                sa[2 * t * tile:(2 * t + 2) * tile], v_ref[...], preferred_element_type=F32
             )
+            return both(sums[:tile] + sums[tile:])
 
         phase = phase + 1
         outgoing = (gz, gx_, gc)
@@ -322,15 +337,13 @@
         updated = jnp.where(
             moved > shrink, moved - shrink, jnp.where(moved < -shrink, moved + shrink, 0.0)
         )
-        following = (1.0 + math.sqrt(1.0 + 4.0 * momentum * momentum)) / 2.0
-        extrapolated = updated + (momentum - 1.0) / following * (updated - current)
+        if iteration + 1 == ITERS:
+            delta_ref[...] = updated - current
+            cur_ref[...] = current
+            break
+        x_ref[...] = updated + weight_of(iteration) * (updated - current)
         cur_ref[...] = updated
-        momentum = following
-        if iteration + 1 < ITERS:
-            x_ref[...] = extrapolated
-            send(phase + 1, order)
-        else:
-            ext_ref[...] = extrapolated
+        send(phase + 1, order)
 
     for phase in range(2 * ITERS):
         for side in SIDES:
@@ -360,7 +373,7 @@
         ]
 
     out = jax.ShapeDtypeStruct(estimate.shape, F32)
-    return pl.pallas_call(
+    delta, current = pl.pallas_call(
         functools.partial(kernel, nx, ny, rows, cols, depth, taps, ranks),
         out_shape=(out, out),
         in_specs=[smem, smem, smem, hbm, hbm, hbm],
@@ -376,18 +389,20 @@
             pltpu.VMEM((ranks, rows + 2 * tall, own), F32),
             pltpu.VMEM((ranks, cols + 2 * wide, own), F32),
             pltpu.VMEM((ranks * own, 8 * own), BF16),
-            pltpu.VMEM((4 * own, 2 * ranks * own), BF16),
+            pltpu.VMEM((8 * own, ranks * own), BF16),
             pltpu.VMEM((ranks, 2 * depth, 2 * depth), BF16),
             pltpu.VMEM((ranks, 2 * depth, 2 * depth), BF16),
             pltpu.VMEM((ranks * own, 2 * depth), F32),
-            pltpu.VMEM((2 * ranks * own, 2 * depth), BF16),
+            pltpu.VMEM((ranks * own, 2 * depth), BF16),
             pltpu.SemaphoreType.DMA((3,)),
             pltpu.SemaphoreType.DMA((phases, len(SIDES))),
             pltpu.SemaphoreType.DMA((phases, len(SIDES))),
         ],
         compiler_params=pltpu.CompilerParams(collective_id=0, has_side_effects=True),
         name="fista",
-    )(kernels, step_size, penalty, estimate, measured, weights)
+    )(kernels.transpose(1, 0, 2), step_size, penalty, estimate, measured, weights)
+    updated = current + delta
+    return updated, updated + weight_of(ITERS - 1) * delta
 
 
 def solution(mesh):

time: 35.4 us -> 32.3 us (0.912)
  local copies, waits for them, and re-layouts: 3.56 us -> 0 us
  other arithmetic: 0 us -> 1.69 us
  Pallas kernels: 29.6 us -> 28.5 us
    unnamed x5 -> x0, local copies, waits for them, and re-layouts: 3.56 us -> none
    add x0 -> x1, other arithmetic: none -> 1.69 us  [on_device(): return (updated, updated + weight_of(ITERS - 1) * delta)]
    pallas_call x1, Pallas kernels: 29.6 us -> 28.5 us  [on_device(): pl.pallas_call(functools.partial(kernel, nx, ny, rows, cols, depth, taps,...]
where the time goes in v1:
time: 32.3 us; the launch traced here: 32.1 us
  Pallas kernels  28.5 us (88%)
  between operations  1.93 us (6%)
  other arithmetic  1.69 us (5%)
    pallas_call x1, Pallas kernels, on_device(): pl.pallas_call(functools.partial(kernel, nx, ny, rows, cols, depth, taps,...  28.5 us
    add x1, other arithmetic, on_device(): return (updated, updated + weight_of(ITERS - 1) * delta)  1.69 us

profile of v1, /device:TPU:1, one launch (start us, length us, event | category | flops | bytes accessed | tf_op | source)
XLA Modules:
  0.0 32.1 jit_solution(9295767870699512651)
XLA Ops:
  1.9 28.5 %fista.1 = (f32[16,16,128]{2,1,0:T(8,128)}, f32[16,16,128]{2,1,0:T(8,128)}) custom-call(f32[3,4,15]{2,1,0:T(4,128)} %bitcast.1, f32[1]{0:T(128)S(6)} %copy.8.step_ref, f32[1]{0:T(128)S(6)} %copy.9.pen_ref, f32[16,16,128]{2,1,0:T(8,128)} %est_ref.1, f32[16,16,128]{2,1,0:T(8,128)} %meas_ref.1, f32[4,16,16,128]{3,2,1,0:T(8,128)} %w_ref.1), custom_call_target="tpu_custom_call" | custom-call | tf_op jit(solution)/shard_map/fista/pallas_call | solution.py:376
  30.4 1.7 %multiply_add_fusion = (f32[16,16,128]{2,1,0:T(8,128)}, f32[16,16,128]{2,1,0:T(8,128)}) fusion(f32[16,16,128]{2,1,0:T(8,128)} %get-tuple-element.5, f32[16,16,128]{2,1,0:T(8,128)} %get-tuple-element.4), kind=kLoop, calls=%fused_computation | loop fusion | flops 98304 | bytes 524288 | tf_op jit(solution)/shard_map/add | solution.py:405

commit v2 on v1

--- a/solution.py
+++ b/solution.py
@@ -10,6 +10,7 @@
 
 ITERS = 2
 SUBLANES = 8
+GRANT = 24 << 20
 MESH = pl.DeviceIdType.MESH
 SIDES = [(0, -1), (0, 1), (-1, 0), (1, 0), (-1, -1), (-1, 1), (1, -1), (1, 1)]
 F32 = jnp.float32
@@ -36,9 +37,9 @@
 
 def kernel(
     nx, ny, rows, cols, depth, taps, ranks,
-    k_ref, step_ref, pen_ref, est_ref, meas_ref, w_ref,
+    step_ref, pen_ref, taps_ref, est_ref, meas_ref, w_ref,
     delta_ref, cur_ref,
-    x_ref, m_ref, wv_ref, hz, hx, hc, gz, gx_, gc,
+    k_ref, x_ref, m_ref, wv_ref, hz, hx, hc, gz, gx_, gc,
     a0, a1, b0, b1, sf, sa, zf, za, acc, v_ref,
     local_sem, send_sem, recv_sem,
 ):
@@ -111,9 +112,7 @@
         pltpu.make_async_copy(meas_ref, m_ref, local_sem.at[1]),
         pltpu.make_async_copy(w_ref, wv_ref, local_sem.at[2]),
     ]
-    for copy in copies:
-        copy.start()
-
+    copies.append(pltpu.make_async_copy(taps_ref, k_ref, local_sem.at[3]))
     barrier = pltpu.get_barrier_semaphore()
     near = 0
     for side in SIDES:
@@ -123,6 +122,8 @@
                 barrier, inc=1, device_id=(gx + side[0], gy + side[1]), device_id_type=MESH
             )
         near = near + there(side).astype(jnp.int32)
+    for copy in copies[::-1]:
+        copy.start()
     pl.semaphore_wait(barrier, near)
     order = SIDES[4:] + SIDES[:4]
     send(0, order)
@@ -141,6 +142,8 @@
             def _():
                 ref = slot(halo, phase, side, phase % 2 == 1)
                 ref[...] = jnp.zeros(ref.shape, F32)
+
+    copies.pop().wait()
 
     tile = own
 
@@ -362,7 +365,7 @@
     assert cols == 2 * wide and rows == 2 * tall and ITERS >= 1
     phases = 2 * ITERS
     smem = pl.BlockSpec(memory_space=pltpu.SMEM)
-    hbm = pl.BlockSpec(memory_space=pl.ANY)
+    hbm = pl.BlockSpec(memory_space=pltpu.HBM)
     vmem = pl.BlockSpec(memory_space=pltpu.VMEM)
 
     def pieces(lead):
@@ -376,9 +379,10 @@
     delta, current = pl.pallas_call(
         functools.partial(kernel, nx, ny, rows, cols, depth, taps, ranks),
         out_shape=(out, out),
-        in_specs=[smem, smem, smem, hbm, hbm, hbm],
+        in_specs=[smem, smem, hbm, hbm, hbm, hbm],
         out_specs=(vmem, vmem),
         scratch_shapes=[
+            pltpu.SMEM((kernels.shape[1], ranks, taps), F32),
             pltpu.VMEM(estimate.shape, F32),
             pltpu.VMEM(measured.shape, F32),
             pltpu.VMEM(weights.shape, F32),
@@ -394,13 +398,22 @@
             pltpu.VMEM((ranks, 2 * depth, 2 * depth), BF16),
             pltpu.VMEM((ranks * own, 2 * depth), F32),
             pltpu.VMEM((ranks * own, 2 * depth), BF16),
-            pltpu.SemaphoreType.DMA((3,)),
+            pltpu.SemaphoreType.DMA((4,)),
             pltpu.SemaphoreType.DMA((phases, len(SIDES))),
             pltpu.SemaphoreType.DMA((phases, len(SIDES))),
         ],
-        compiler_params=pltpu.CompilerParams(collective_id=0, has_side_effects=True),
+        compiler_params=pltpu.CompilerParams(
+            collective_id=0, has_side_effects=True, vmem_limit_bytes=GRANT
+        ),
         name="fista",
-    )(kernels.transpose(1, 0, 2), step_size, penalty, estimate, measured, weights)
+    )(
+        step_size,
+        penalty,
+        *(
+            pltpu.with_memory_space_constraint(array, pltpu.HBM)
+            for array in (kernels.transpose(1, 0, 2), estimate, measured, weights)
+        ),
+    )
     updated = current + delta
     return updated, updated + weight_of(ITERS - 1) * delta
 

time: 32.3 us -> 29.8 us (0.923)
  Pallas kernels: 28.5 us -> 27 us
  other arithmetic: 1.69 us -> 0.72 us
    pallas_call x1, Pallas kernels: 28.5 us -> 27 us  [on_device(): pl.pallas_call(functools.partial(kernel, nx, ny, rows, cols, depth, taps,...]
    add x1, other arithmetic: 1.69 us -> 0.72 us  [on_device(): return (updated, updated + weight_of(ITERS - 1) * delta)]
where the time goes in v2:
time: 29.8 us; the launch traced here: 29.7 us
  Pallas kernels  27 us (91%)
  between operations  1.93 us (6%)
  other arithmetic  0.72 us (2%)
    pallas_call x1, Pallas kernels, on_device(): pl.pallas_call(functools.partial(kernel, nx, ny, rows, cols, depth, taps,...  27 us
    add x1, other arithmetic, on_device(): return (updated, updated + weight_of(ITERS - 1) * delta)  0.72 us

profile of v2, /device:TPU:1, one launch (start us, length us, event | category | flops | bytes accessed | tf_op | source)
XLA Modules:
  0.0 29.7 jit_solution(4106614749485648488)
XLA Ops:
  1.9 27.0 %fista.1 = (f32[16,16,128]{2,1,0:T(8,128)S(1)}, f32[16,16,128]{2,1,0:T(8,128)S(1)}) custom-call(f32[1]{0:T(128)S(6)} %copy.8.step_ref, f32[1]{0:T(128)S(6)} %copy.9.pen_ref, f32[3,4,15]{2,1,0:T(4,128)} %bitcast.1, f32[16,16,128]{2,1,0:T(8,128)} %est_ref.1, f32[16,16,128]{2,1,0:T(8,128)} %meas_ref.1, f32[4,16,16,128]{3,2,1,0:T(8,128)} %w_ref.1), custom_call_target="tpu_custom_call" | custom-call | tf_op jit(solution)/shard_map/fista/pallas_call | solution.py:379
  29.0 0.7 %multiply_add_fusion = (f32[16,16,128]{2,1,0:T(8,128)}, f32[16,16,128]{2,1,0:T(8,128)}) fusion(f32[16,16,128]{2,1,0:T(8,128)S(1)} %get-tuple-element.5, f32[16,16,128]{2,1,0:T(8,128)S(1)} %get-tuple-element.4), kind=kLoop, calls=%fused_computation | loop fusion | flops 98304 | bytes 524288 | tf_op jit(solution)/shard_map/add | solution.py:418

commit v3 on v2

--- a/solution.py
+++ b/solution.py
@@ -125,7 +125,7 @@
     for copy in copies[::-1]:
         copy.start()
     pl.semaphore_wait(barrier, near)
-    order = SIDES[4:] + SIDES[:4]
+    order = SIDES[:2] + SIDES[4:] + SIDES[2:4]
     send(0, order)
 
     spare = (slice(0, wide - margin), slice(margin, wide))
@@ -264,7 +264,6 @@
             put(3, n * tall * wide + u * 2 * wide, (first, first + 1), flanks[n % 2])
         return 0
 
-    lax.fori_loop(0, rows, fill_own, 0)
     lax.fori_loop(0, rows // 2, fill_z, 0)
     lax.fori_loop(0, tall, fill_x, 0)
     lax.fori_loop(0, tall // 2, fill_c, 0)
@@ -320,6 +319,8 @@
             ref = outgoing[t - 1]
             ref[iteration] = spread(t).reshape(ref.shape[1:])
             send(phase, groups[t])
+        if iteration == 0:
+            lax.fori_loop(0, rows, fill_own, 0)
         acc[:own, :depth] = spread(0)
         grad = acc.at[:own, :depth]
         receive(phase, SIDES)

time: 29.8 us -> 29.2 us (0.980)
  the two profiles are of different devices: /device:TPU:1 before, /device:TPU:3 now
where the time goes in v3:
time: 29.2 us; the launch traced here: 29.1 us
  Pallas kernels  26.4 us (90%)
  between operations  1.93 us (7%)
  other arithmetic  0.72 us (2%)
    pallas_call x1, Pallas kernels, on_device(): pl.pallas_call(functools.partial(kernel, nx, ny, rows, cols, depth, taps,...  26.4 us
    add x1, other arithmetic, on_device(): return (updated, updated + weight_of(ITERS - 1) * delta)  0.72 us

profile of v3, /device:TPU:3, one launch (start us, length us, event | category | flops | bytes accessed | tf_op | source)
XLA Modules:
  0.0 29.1 jit_solution(2578271229543974192)
XLA Ops:
  1.9 26.4 %fista.1 = (f32[16,16,128]{2,1,0:T(8,128)S(1)}, f32[16,16,128]{2,1,0:T(8,128)S(1)}) custom-call(f32[1]{0:T(128)S(6)} %copy.8.step_ref, f32[1]{0:T(128)S(6)} %copy.9.pen_ref, f32[3,4,15]{2,1,0:T(4,128)} %bitcast.1, f32[16,16,128]{2,1,0:T(8,128)} %est_ref.1, f32[16,16,128]{2,1,0:T(8,128)} %meas_ref.1, f32[4,16,16,128]{3,2,1,0:T(8,128)} %w_ref.1), custom_call_target="tpu_custom_call" | custom-call | tf_op jit(solution)/shard_map/fista/pallas_call | solution.py:380
  28.3 0.7 %multiply_add_fusion = (f32[16,16,128]{2,1,0:T(8,128)}, f32[16,16,128]{2,1,0:T(8,128)}) fusion(f32[16,16,128]{2,1,0:T(8,128)S(1)} %get-tuple-element.5, f32[16,16,128]{2,1,0:T(8,128)S(1)} %get-tuple-element.4), kind=kLoop, calls=%fused_computation | loop fusion | flops 98304 | bytes 524288 | tf_op jit(solution)/shard_map/add | solution.py:419
